TPU v7x, 512 devices: a whole 4x4x16 slice. The times are simulated.
512 devices in a mesh: row: 16 (over x, y), col: 32 (over z, core).
Axes of the slice: x: 4, y: 4, z: 16, core: 2. Of those that a mesh axis runs over, the one named last changes fastest.
Arguments:
- front: bfloat16 [16384, 16384], P('row', 'col'), may hold values from -0.046875 to 0.046875
- diag_inverse: float32 [128, 128, 128], P('row'), may hold values from -0.25 to 1.5
- load: float32 [8, 16384], P(None, 'row'), may hold values from -6 to 6
- panel_order: int32 [128], replicated, may hold values from 0 to 127, each once
- tie: float32 [32, 16384], P('col', 'row'), may hold values from 0.5 to 1.5
- mass: float32 [32, 16384], P('col', 'row'), may hold values from 0.5 to 6
- modes: bfloat16 [1024, 32, 16384], P(None, 'col', 'row'), may hold values from -0.0234375 to 0.0234375
Outputs:
- front_solution: float32 [8, 16384], P(None, 'row')
- residual_vectors: float32 [8, 32, 16384], P(None, 'col', 'row')
All inputs are finite; a program needn't handle non-finite values.
Results may differ from a plain program's by a relative error of at most 0.0049.
Values may be sent and summed in bfloat16 or wider, within the bound.
No kernel may reach another device: no remote copies, remote signals or barrier semaphores. Data moves between devices by JAX's collectives and lax.ppermute only.
A program may use at most 64 MiB of HBM per device.

v0:
```python
import jax
import jax.numpy as jnp
from jax import lax
from jax.sharding import PartitionSpec as P

LEVELS = 4
highest = lax.Precision.HIGHEST


def on_device(front, diag_inverse, load, panel_order, tie, mass, modes):
    vectors = load.shape[0]
    block_size = diag_inverse.shape[1]
    local_panels = diag_inverse.shape[0]
    rows_local = front.shape[0]
    cols_local = front.shape[1]
    panels = panel_order.shape[0]
    row_at = lax.axis_index("row")
    col_at = lax.axis_index("col")
    counting = jnp.arange(panels, dtype=jnp.int32)
    matches = panel_order[:, None] == counting[None, :]
    ranks = jnp.sum(jnp.where(matches, counting[:, None], 0), axis=0)
    levels_of = ranks // (panels // LEVELS)
    position_level = jnp.repeat(levels_of, block_size)
    row_level = lax.dynamic_slice_in_dim(position_level, row_at * rows_local, rows_local, 0)
    pending = jnp.zeros((vectors, rows_local), jnp.float32)
    forward_out = jnp.zeros((vectors, rows_local), jnp.float32)
    for level in range(LEVELS):
        if level > 0:
            total_sum = lax.psum(pending, "col")
        else:
            total_sum = pending
        remain = (load - total_sum).reshape(vectors, local_panels, block_size)
        candidate = jnp.einsum("vpj,pij->vpi", remain, diag_inverse, precision=highest).reshape(
            vectors, rows_local
        )
        chosen = row_level[None, :] == level
        forward_out = jnp.where(chosen, candidate, forward_out)
        if level < LEVELS - 1:
            fresh = jnp.where(chosen, forward_out, 0.0).astype(jnp.bfloat16)
            whole = lax.all_gather(fresh, "row", axis=1, tiled=True)
            mine = lax.dynamic_slice_in_dim(whole, col_at * cols_local, cols_local, 1)
            pending = pending + jnp.dot(mine, front.T, preferred_element_type=jnp.float32)
    back_pending = jnp.zeros((vectors, cols_local), jnp.float32)
    back_out = jnp.zeros((vectors, rows_local), jnp.float32)
    for level in reversed(range(LEVELS)):
        if level < LEVELS - 1:
            column_sum = lax.psum(back_pending, "row")
            full_sum = lax.all_gather(column_sum, "col", axis=1, tiled=True)
            here = lax.dynamic_slice_in_dim(full_sum, row_at * rows_local, rows_local, 1)
        else:
            here = jnp.zeros((vectors, rows_local), jnp.float32)
        remain = (forward_out - here).reshape(vectors, local_panels, block_size)
        candidate = jnp.einsum("vpj,pji->vpi", remain, diag_inverse, precision=highest).reshape(
            vectors, rows_local
        )
        chosen = row_level[None, :] == level
        back_out = jnp.where(chosen, candidate, back_out)
        if level > 0:
            fresh = jnp.where(chosen, back_out, 0.0).astype(jnp.bfloat16)
            back_pending = back_pending + jnp.dot(fresh, front, preferred_element_type=jnp.float32)
    static = tie[None, :, :] * back_out[:, None, :]
    weighted = (mass[None, :, :] * static).astype(jnp.bfloat16).reshape(vectors, -1)
    mode_rows = modes.reshape(modes.shape[0], -1)
    partial_coords = lax.dot_general(
        weighted, mode_rows, (((1,), (1,)), ((), ())), preferred_element_type=jnp.float32
    )
    coords = lax.psum(partial_coords, ("row", "col"))
    correction = jnp.dot(coords.astype(jnp.bfloat16), mode_rows, preferred_element_type=jnp.float32)
    return (back_out, static - correction.reshape(static.shape))


def solution(mesh):
    in_specs = (
        P("row", "col"),
        P("row", None, None),
        P(None, "row"),
        P(),
        P("col", "row"),
        P("col", "row"),
        P(None, "col", "row"),
    )
    out_specs = (P(None, "row"), P(None, "col", "row"))
    return jax.shard_map(
        on_device, mesh=mesh, in_specs=in_specs, out_specs=out_specs, check_vma=False
    )
```

profile of v0, /device:TPU:1, one launch (start us, length us, event | category | flops | bytes accessed | tf_op | source)
XLA Modules:
  0.0 765.4 jit_solution(5559178636949547583)
XLA Ops:
  0.7 0.9 select_reduce_fusion
  1.6 0.1 broadcast_bitcast_fusion
  1.7 2.0 select_convert_fusion.5
  3.7 19.7 %all_gather.18 = bf16[8,16384]{1,0:T(8,128)(2,1)S(1)} all-gather(bf16[8,1024]{1,0:T(8,128)(2,1)S(1)} %get-tuple-element.14), channel_id=1, replica_groups=mesh['row'=16,'col'=32] {'row'}, dimensions={1}, use_global_device_ids=true | all-gather | bytes 278528 | tf_op jit(solution)/shard_map/all_gather | solution.py:40
  23.3 1.6 fusion.64
  24.9 99.0 %psum.49 = f32[8,1024]{1,0:T(8,128)S(1)} all-reduce(f32[8,1024]{1,0:T(8,128)S(1)} %fusion.64), channel_id=1, replica_groups=mesh['row'=16,'col'=32] {'col'}, use_global_device_ids=true, to_apply=%region_1.2 | all-reduce | flops 8192 | bytes 65536 | tf_op jit(solution)/shard_map/psum | solution.py:29
  123.9 2.0 select_convert_fusion.4
  125.9 17.9 %all_gather.19 = bf16[8,16384]{1,0:T(8,128)(2,1)S(1)} all-gather(bf16[8,1024]{1,0:T(8,128)(2,1)S(1)} %get-tuple-element.8), channel_id=1, replica_groups=mesh['row'=16,'col'=32] {'row'}, dimensions={1}, use_global_device_ids=true | all-gather | bytes 278528 | tf_op jit(solution)/shard_map/all_gather | solution.py:40
  143.8 0.4 convolution_add_fusion.1
  144.2 95.2 %psum.50 = f32[8,1024]{1,0:T(8,128)S(1)} all-reduce(f32[8,1024]{1,0:T(8,128)S(1)} %convolution_add_fusion.1), channel_id=1, replica_groups=mesh['row'=16,'col'=32] {'col'}, use_global_device_ids=true, to_apply=%region_2.3 | all-reduce | flops 8192 | bytes 65536 | tf_op jit(solution)/shard_map/psum | solution.py:29
  239.4 2.0 select_convert_fusion.3
  241.4 16.6 %all_gather.20 = bf16[8,16384]{1,0:T(8,128)(2,1)S(1)} all-gather(bf16[8,1024]{1,0:T(8,128)(2,1)S(1)} %get-tuple-element.17), channel_id=1, replica_groups=mesh['row'=16,'col'=32] {'row'}, dimensions={1}, use_global_device_ids=true | all-gather | bytes 278528 | tf_op jit(solution)/shard_map/all_gather | solution.py:40
  258.0 0.4 convolution_add_fusion
  258.4 94.9 %psum.51 = f32[8,1024]{1,0:T(8,128)S(1)} all-reduce(f32[8,1024]{1,0:T(8,128)S(1)} %convolution_add_fusion), channel_id=1, replica_groups=mesh['row'=16,'col'=32] {'col'}, use_global_device_ids=true, to_apply=%region_3.4 | all-reduce | flops 8192 | bytes 65536 | tf_op jit(solution)/shard_map/psum | solution.py:29
  353.3 2.0 bitcast_select_fusion.5
  355.3 1.6 fusion.22
  356.9 0.2 fusion.40
  357.1 58.2 %psum.52 = f32[8,512]{1,0:T(8,128)S(1)} all-reduce(f32[8,512]{1,0:T(8,128)S(1)} %fusion.40), channel_id=1, replica_groups=mesh['row'=16,'col'=32] {'row'}, use_global_device_ids=true, to_apply=%region_4.5 | all-reduce | flops 4096 | bytes 32768 | tf_op jit(solution)/shard_map/psum | solution.py:47
  415.3 45.4 %all_gather.21 = f32[8,16384]{1,0:T(8,128)S(1)} all-gather(f32[8,512]{1,0:T(8,128)S(1)} %psum.52), channel_id=1, replica_groups=mesh['row'=16,'col'=32] {'col'}, dimensions={1}, use_global_device_ids=true | all-gather | bytes 540672 | tf_op jit(solution)/shard_map/all_gather | solution.py:48
  460.8 1.6 bitcast_select_fusion.3
  462.3 0.2 convolution_add_fusion.3
  462.6 55.9 %psum.53 = f32[8,512]{1,0:T(8,128)S(1)} all-reduce(f32[8,512]{1,0:T(8,128)S(1)} %convolution_add_fusion.3), channel_id=1, replica_groups=mesh['row'=16,'col'=32] {'row'}, use_global_device_ids=true, to_apply=%region_5.6 | all-reduce | flops 4096 | bytes 32768 | tf_op jit(solution)/shard_map/psum | solution.py:47
  518.5 44.6 %all_gather.22 = f32[8,16384]{1,0:T(8,128)S(1)} all-gather(f32[8,512]{1,0:T(8,128)S(1)} %psum.53), channel_id=1, replica_groups=mesh['row'=16,'col'=32] {'col'}, dimensions={1}, use_global_device_ids=true | all-gather | bytes 540672 | tf_op jit(solution)/shard_map/all_gather | solution.py:48
  563.1 1.6 fusion.18
  564.6 0.2 convolution_add_fusion.2
  564.9 55.8 %psum.54 = f32[8,512]{1,0:T(8,128)S(1)} all-reduce(f32[8,512]{1,0:T(8,128)S(1)} %convolution_add_fusion.2), channel_id=1, replica_groups=mesh['row'=16,'col'=32] {'row'}, use_global_device_ids=true, to_apply=%region_6.7 | all-reduce | flops 4096 | bytes 32768 | tf_op jit(solution)/shard_map/psum | solution.py:47
  620.6 42.0 %all_gather.23 = f32[8,16384]{1,0:T(8,128)S(1)} all-gather(f32[8,512]{1,0:T(8,128)S(1)} %psum.54), channel_id=1, replica_groups=mesh['row'=16,'col'=32] {'col'}, dimensions={1}, use_global_device_ids=true | all-gather | bytes 540672 | tf_op jit(solution)/shard_map/all_gather | solution.py:48
  662.6 1.6 bitcast_select_fusion.1
  664.2 0.6 fusion.2
  664.8 99.5 %psum.55 = bf16[8,1024]{1,0:T(8,128)(2,1)S(1)} all-reduce(f32[8,1024]{1,0:T(8,128)S(1)} %fusion.2), channel_id=1, replica_groups=mesh['row'=16,'col'=32] {'row','col'}, use_global_device_ids=true, to_apply=%region_7.8 | all-reduce | flops 8192 | bytes 49152 | tf_op jit(solution)/shard_map/psum | solution.py:67
  764.4 0.4 fusion.7
  764.8 0.7 copy.11
  (14 shorter events, 0.1 us)
Async XLA Ops:
  0.6 663.6 %copy-start = (bf16[1024,1,1024]{2,0,1:T(8,128)(2,1)S(1)}, bf16[1024,1,1024]{2,0,1:T(8,128)(2,1)}, u32[]{:S(2)}) copy-start(bf16[1024,1,1024]{2,0,1:T(8,128)(2,1)} %param.13) | copy-start | bytes 6291460
  0.6 143.2 %copy-start.1 = (bf16[1024,512]{1,0:T(8,128)(2,1)S(1)}, bf16[1024,512]{1,0:T(8,128)(2,1)}, u32[]{:S(2)}) copy-start(bf16[1024,512]{1,0:T(8,128)(2,1)} %param.7) | copy-start | bytes 3145732
  0.7 123.3 %copy-start.2 = (f32[8,1024]{1,0:T(8,128)S(1)}, f32[8,1024]{1,0:T(8,128)}, u32[]{:S(2)}) copy-start(f32[8,1024]{1,0:T(8,128)} %param.9) | copy-start | bytes 98308
  462.6 201.6 %copy-start.4 = (f32[1,1024]{1,0:T(1,128)S(1)}, f32[1,1024]{1,0:T(1,128)}, u32[]{:S(2)}) copy-start(f32[1,1024]{1,0:T(1,128)} %param.11) | copy-start | bytes 12292
  462.6 201.6 %copy-start.5 = (f32[1,1024]{1,0:T(1,128)S(1)}, f32[1,1024]{1,0:T(1,128)}, u32[]{:S(2)}) copy-start(f32[1,1024]{1,0:T(1,128)} %param.12) | copy-start | bytes 12292
  664.2 100.6 %copy-start.3 = (f32[8,1024]{1,0:T(8,128)}, f32[8,1024]{1,0:T(8,128)S(1)}, u32[]{:S(2)}) copy-start(f32[8,1024]{1,0:T(8,128)S(1)} %get-tuple-element.23) | copy-start | bytes 98308
where the time goes:
time: 766 us; the launch traced here: 765 us
  blocking collectives  745 us (97%)
  matrix products  18.2 us (2%)
    psum x3, blocking collectives, on_device(): total_sum = lax.psum(pending, 'col')  289 us
    psum x3, blocking collectives, on_device(): column_sum = lax.psum(back_pending, 'row')  170 us
    all_gather x3, blocking collectives, on_device(): full_sum = lax.all_gather(column_sum, 'col', axis=1, tiled=True)  132 us
    psum x1, blocking collectives, on_device(): coords = lax.psum(partial_coords, ('row', 'col'))  99.5 us
    all_gather x3, blocking collectives, on_device(): whole = lax.all_gather(fresh, 'row', axis=1, tiled=True)  54.2 us

commit v1 on v0

--- a/solution.py
+++ b/solution.py
@@ -64,7 +64,7 @@
     partial_coords = lax.dot_general(
         weighted, mode_rows, (((1,), (1,)), ((), ())), preferred_element_type=jnp.float32
     )
-    coords = lax.psum(partial_coords, ("row", "col"))
+    coords = lax.psum(lax.psum(partial_coords, "row"), "col")
     correction = jnp.dot(coords.astype(jnp.bfloat16), mode_rows, preferred_element_type=jnp.float32)
     return (back_out, static - correction.reshape(static.shape))
 

time: 766 us -> 823 us (1.074)
  blocking collectives: 745 us -> 801 us
    psum x1 -> x2, blocking collectives: 99.5 us -> 156 us  [on_device(): coords = lax.psum(lax.psum(partial_coords, 'row'), 'col')]
where the time goes in v1:
time: 823 us; the launch traced here: 822 us
  blocking collectives  801 us (97%)
  matrix products  18.2 us (2%)
    psum x3, blocking collectives, on_device(): total_sum = lax.psum(pending, 'col')  289 us
    psum x3, blocking collectives, on_device(): column_sum = lax.psum(back_pending, 'row')  170 us
    psum x2, blocking collectives, on_device(): coords = lax.psum(lax.psum(partial_coords, 'row'), 'col')  156 us
    all_gather x3, blocking collectives, on_device(): full_sum = lax.all_gather(column_sum, 'col', axis=1, tiled=True)  132 us
    all_gather x3, blocking collectives, on_device(): whole = lax.all_gather(fresh, 'row', axis=1, tiled=True)  54.2 us

profile of v1, /device:TPU:1, one launch (start us, length us, event | category | flops | bytes accessed | tf_op | source)
XLA Modules:
  0.0 822.1 jit_solution(5408746188882743132)
XLA Ops:
  0.7 0.9 select_reduce_fusion
  1.7 2.0 select_convert_fusion.5
  3.7 19.7 %all_gather.18 = bf16[8,16384]{1,0:T(8,128)(2,1)S(1)} all-gather(bf16[8,1024]{1,0:T(8,128)(2,1)S(1)} %get-tuple-element.14), channel_id=1, replica_groups=mesh['row'=16,'col'=32] {'row'}, dimensions={1}, use_global_device_ids=true | all-gather | bytes 278528 | tf_op jit(solution)/shard_map/all_gather | solution.py:40
  23.3 1.6 fusion.64
  24.9 99.0 %psum.56 = f32[8,1024]{1,0:T(8,128)S(1)} all-reduce(f32[8,1024]{1,0:T(8,128)S(1)} %fusion.64), channel_id=1, replica_groups=mesh['row'=16,'col'=32] {'col'}, use_global_device_ids=true, to_apply=%region_1.2 | all-reduce | flops 8192 | bytes 65536 | tf_op jit(solution)/shard_map/psum | solution.py:29
  123.9 2.0 select_convert_fusion.4
  125.9 17.9 %all_gather.19 = bf16[8,16384]{1,0:T(8,128)(2,1)S(1)} all-gather(bf16[8,1024]{1,0:T(8,128)(2,1)S(1)} %get-tuple-element.8), channel_id=1, replica_groups=mesh['row'=16,'col'=32] {'row'}, dimensions={1}, use_global_device_ids=true | all-gather | bytes 278528 | tf_op jit(solution)/shard_map/all_gather | solution.py:40
  143.8 0.4 convolution_add_fusion.1
  144.2 95.2 %psum.57 = f32[8,1024]{1,0:T(8,128)S(1)} all-reduce(f32[8,1024]{1,0:T(8,128)S(1)} %convolution_add_fusion.1), channel_id=1, replica_groups=mesh['row'=16,'col'=32] {'col'}, use_global_device_ids=true, to_apply=%region_2.3 | all-reduce | flops 8192 | bytes 65536 | tf_op jit(solution)/shard_map/psum | solution.py:29
  239.4 2.0 select_convert_fusion.3
  241.4 16.6 %all_gather.20 = bf16[8,16384]{1,0:T(8,128)(2,1)S(1)} all-gather(bf16[8,1024]{1,0:T(8,128)(2,1)S(1)} %get-tuple-element.17), channel_id=1, replica_groups=mesh['row'=16,'col'=32] {'row'}, dimensions={1}, use_global_device_ids=true | all-gather | bytes 278528 | tf_op jit(solution)/shard_map/all_gather | solution.py:40
  258.0 0.4 convolution_add_fusion
  258.4 94.9 %psum.58 = f32[8,1024]{1,0:T(8,128)S(1)} all-reduce(f32[8,1024]{1,0:T(8,128)S(1)} %convolution_add_fusion), channel_id=1, replica_groups=mesh['row'=16,'col'=32] {'col'}, use_global_device_ids=true, to_apply=%region_3.4 | all-reduce | flops 8192 | bytes 65536 | tf_op jit(solution)/shard_map/psum | solution.py:29
  353.3 2.0 bitcast_select_fusion.5
  355.3 1.6 fusion.22
  356.9 0.2 fusion.40
  357.1 58.2 %psum.59 = f32[8,512]{1,0:T(8,128)S(1)} all-reduce(f32[8,512]{1,0:T(8,128)S(1)} %fusion.40), channel_id=1, replica_groups=mesh['row'=16,'col'=32] {'row'}, use_global_device_ids=true, to_apply=%region_4.5 | all-reduce | flops 4096 | bytes 32768 | tf_op jit(solution)/shard_map/psum | solution.py:47
  415.3 45.4 %all_gather.21 = f32[8,16384]{1,0:T(8,128)S(1)} all-gather(f32[8,512]{1,0:T(8,128)S(1)} %psum.59), channel_id=1, replica_groups=mesh['row'=16,'col'=32] {'col'}, dimensions={1}, use_global_device_ids=true | all-gather | bytes 540672 | tf_op jit(solution)/shard_map/all_gather | solution.py:48
  460.8 1.6 bitcast_select_fusion.3
  462.3 0.2 convolution_add_fusion.3
  462.6 55.9 %psum.60 = f32[8,512]{1,0:T(8,128)S(1)} all-reduce(f32[8,512]{1,0:T(8,128)S(1)} %convolution_add_fusion.3), channel_id=1, replica_groups=mesh['row'=16,'col'=32] {'row'}, use_global_device_ids=true, to_apply=%region_5.6 | all-reduce | flops 4096 | bytes 32768 | tf_op jit(solution)/shard_map/psum | solution.py:47
  518.5 44.6 %all_gather.22 = f32[8,16384]{1,0:T(8,128)S(1)} all-gather(f32[8,512]{1,0:T(8,128)S(1)} %psum.60), channel_id=1, replica_groups=mesh['row'=16,'col'=32] {'col'}, dimensions={1}, use_global_device_ids=true | all-gather | bytes 540672 | tf_op jit(solution)/shard_map/all_gather | solution.py:48
  563.1 1.6 fusion.18
  564.6 0.2 convolution_add_fusion.2
  564.9 55.8 %psum.61 = f32[8,512]{1,0:T(8,128)S(1)} all-reduce(f32[8,512]{1,0:T(8,128)S(1)} %convolution_add_fusion.2), channel_id=1, replica_groups=mesh['row'=16,'col'=32] {'row'}, use_global_device_ids=true, to_apply=%region_6.7 | all-reduce | flops 4096 | bytes 32768 | tf_op jit(solution)/shard_map/psum | solution.py:47
  620.6 42.0 %all_gather.23 = f32[8,16384]{1,0:T(8,128)S(1)} all-gather(f32[8,512]{1,0:T(8,128)S(1)} %psum.61), channel_id=1, replica_groups=mesh['row'=16,'col'=32] {'col'}, dimensions={1}, use_global_device_ids=true | all-gather | bytes 540672 | tf_op jit(solution)/shard_map/all_gather | solution.py:48
  662.6 1.6 bitcast_select_fusion.1
  664.2 0.6 fusion.2
  664.8 55.8 %psum.62 = f32[8,1024]{1,0:T(8,128)S(1)} all-reduce(f32[8,1024]{1,0:T(8,128)S(1)} %fusion.2), channel_id=1, replica_groups=mesh['row'=16,'col'=32] {'row'}, use_global_device_ids=true, to_apply=%region_7.8 | all-reduce | flops 8192 | bytes 65536 | tf_op jit(solution)/shard_map/psum | solution.py:67
  720.6 100.4 %psum.63 = bf16[8,1024]{1,0:T(8,128)(2,1)S(1)} all-reduce(f32[8,1024]{1,0:T(8,128)S(1)} %psum.62), channel_id=1, replica_groups=mesh['row'=16,'col'=32] {'col'}, use_global_device_ids=true, to_apply=%region_8.9 | all-reduce | flops 8192 | bytes 49152 | tf_op jit(solution)/shard_map/psum | solution.py:67
  821.0 0.4 fusion.7
  821.4 0.7 copy.11
  (15 shorter events, 0.1 us)
Async XLA Ops:
  0.6 663.6 %copy-start = (bf16[1024,1,1024]{2,0,1:T(8,128)(2,1)S(1)}, bf16[1024,1,1024]{2,0,1:T(8,128)(2,1)}, u32[]{:S(2)}) copy-start(bf16[1024,1,1024]{2,0,1:T(8,128)(2,1)} %param.13) | copy-start | bytes 6291460
  0.6 143.2 %copy-start.1 = (bf16[1024,512]{1,0:T(8,128)(2,1)S(1)}, bf16[1024,512]{1,0:T(8,128)(2,1)}, u32[]{:S(2)}) copy-start(bf16[1024,512]{1,0:T(8,128)(2,1)} %param.7) | copy-start | bytes 3145732
  0.7 123.3 %copy-start.2 = (f32[8,1024]{1,0:T(8,128)S(1)}, f32[8,1024]{1,0:T(8,128)}, u32[]{:S(2)}) copy-start(f32[8,1024]{1,0:T(8,128)} %param.9) | copy-start | bytes 98308
  462.6 201.6 %copy-start.4 = (f32[1,1024]{1,0:T(1,128)S(1)}, f32[1,1024]{1,0:T(1,128)}, u32[]{:S(2)}) copy-start(f32[1,1024]{1,0:T(1,128)} %param.11) | copy-start | bytes 12292
  462.6 201.6 %copy-start.5 = (f32[1,1024]{1,0:T(1,128)S(1)}, f32[1,1024]{1,0:T(1,128)}, u32[]{:S(2)}) copy-start(f32[1,1024]{1,0:T(1,128)} %param.12) | copy-start | bytes 12292
  664.2 157.2 %copy-start.3 = (f32[8,1024]{1,0:T(8,128)}, f32[8,1024]{1,0:T(8,128)S(1)}, u32[]{:S(2)}) copy-start(f32[8,1024]{1,0:T(8,128)S(1)} %get-tuple-element.23) | copy-start | bytes 98308
